TPU v7x, 128 devices: a whole 4x4x4 slice. The times are simulated.
128 devices in a mesh: row: 16 (over y, x), col: 4 (over z), dp: 2 (over core).
Axes of the slice: x: 4, y: 4, z: 4, core: 2. Of those that a mesh axis runs over, the one named last changes fastest.
Arguments:
- inputs: bfloat16 [1024, 8192], P(('col', 'dp'), 'row'), may hold values from -6 to 6
- gate_weight: bfloat16 [8192, 14336], P('row', 'col'), may hold values from -0.0625 to 0.0625
- up_weight: bfloat16 [8192, 14336], P('row', 'col'), may hold values from -0.0625 to 0.0625
- down_weight: bfloat16 [14336, 8192], P('col', 'row'), may hold values from -0.046875 to 0.046875
- reward_head: bfloat16 [8192], P('row'), may hold values from -0.0625 to 0.0625
- upstream: bfloat16 [1024, 8192], P(('col', 'dp'), 'row'), may hold values from -0.59765625 to 0.59765625
- labels: int32 [1024], P(('col', 'dp')), may hold values from 0 to 1
- label_mask: int32 [1024], P(('col', 'dp')), may hold values 0 or 1
Outputs:
- gate_grad: float32 [8192, 14336], P(('row', 'dp'), 'col')
- up_grad: float32 [8192, 14336], P(('row', 'dp'), 'col')
- down_grad: float32 [14336, 8192], P(('col', 'dp'), 'row')
- input_grad: float32 [1024, 8192], P(('col', 'dp'), 'row')
All inputs are finite; a program needn't handle non-finite values. No bound on the sum of `label_mask` on one device may be relied on, other than what follows from the above.
Results may differ from a plain program's by a relative error of at most 0.035.
Values may be sent and summed in bfloat16 or wider, within the bound.
No kernel may reach another device: no remote copies, remote signals or barrier semaphores. Data moves between devices by JAX's collectives and lax.ppermute only.
A program may use at most 128 MiB of HBM per device.

v0:
```python
import jax
import jax.numpy as jnp
from jax import lax
from jax.sharding import PartitionSpec as P

reward_weight = 8.0
BF = jnp.bfloat16
F32 = jnp.float32


def transpose_product(left, right):
    return lax.dot_general(left, right, (((0,), (0,)), ((), ())), preferred_element_type=F32)


def right_transpose(left, right):
    return lax.dot_general(left, right, (((1,), (1,)), ((), ())), preferred_element_type=F32)


def per_device(
    inputs, gate_weight, up_weight, down_weight, reward_head, upstream, labels, label_mask
):
    tokens, depth = inputs.shape
    half = gate_weight.shape[1] // 2
    n_row = lax.axis_size("row")
    core = lax.axis_index("dp")
    row = lax.axis_index("row")
    token_axes = ("col", "dp")
    tags = jnp.stack([labels, label_mask], axis=1).astype(BF)
    tags = jnp.pad(tags, ((0, 0), (0, 126)))
    packed = jnp.concatenate([inputs, upstream, tags], axis=1)
    everyone = lax.all_gather(packed, token_axes, axis=0, tiled=True)
    x_all = everyone[:, :depth]
    upstream_all = everyone[:, depth : 2 * depth]
    total = x_all.shape[0]
    mine = total // n_row
    gate_half = lax.dynamic_slice_in_dim(gate_weight, core * half, half, 1)
    up_half = lax.dynamic_slice_in_dim(up_weight, core * half, half, 1)
    down_half = lax.dynamic_slice_in_dim(down_weight, core * half, half, 0)
    head_value = reward_head.astype(F32)
    head_hidden = jnp.dot(down_half.astype(F32), head_value, precision=lax.Precision.HIGHEST)
    head_inputs = jnp.dot(x_all.astype(F32), head_value, precision=lax.Precision.HIGHEST)
    per_token = half // mine
    extras = jnp.concatenate(
        [
            head_inputs[:, None],
            jnp.tile(head_hidden.reshape(mine, per_token), (n_row, 1)),
            jnp.zeros((total, 127 - per_token), F32),
        ],
        axis=1,
    )
    partial = jnp.concatenate(
        [
            jnp.dot(x_all, gate_half, preferred_element_type=F32).astype(BF),
            jnp.dot(x_all, up_half, preferred_element_type=F32).astype(BF),
            right_transpose(upstream_all, down_half).astype(BF),
            extras.astype(BF),
        ],
        axis=1,
    )
    summed = lax.psum_scatter(partial, "row", scatter_dimension=0, tiled=True).astype(F32)
    gate = summed[:, :half]
    upper = summed[:, half : 2 * half]
    grad_upstream = summed[:, 2 * half : 3 * half]
    extra = summed[:, 3 * half :]
    head_hidden = extra[:, 1 : 1 + per_token].reshape(half)
    sigmoid_gate = jax.nn.sigmoid(gate)
    hidden = (gate * sigmoid_gate * upper).astype(BF)
    score = extra[:, 0] + lax.psum(
        jnp.sum(hidden.astype(F32) * head_hidden[None, :], axis=1), token_axes
    )
    own_tags = lax.dynamic_slice_in_dim(everyone[:, 2 * depth :], row * mine, mine, 0).astype(F32)
    slope = reward_weight * own_tags[:, 1] * (jax.nn.sigmoid(score) - own_tags[:, 0])
    grad_hidden = grad_upstream + slope[:, None] * head_hidden[None, :]
    grad_gate = (grad_hidden * upper * sigmoid_gate * (1.0 + gate * (1.0 - sigmoid_gate))).astype(
        BF
    )
    grad_upper = (grad_hidden * gate * sigmoid_gate).astype(BF)
    slope_high = slope.astype(BF)
    slope_low = (slope - slope_high.astype(F32)).astype(BF)
    slopes = jnp.pad(jnp.stack([slope_high, slope_low], axis=1), ((0, 0), (0, 126)))
    gathered = lax.all_gather(
        jnp.concatenate([hidden, grad_gate, grad_upper, slopes], axis=1), "row", axis=0, tiled=True
    )
    hidden_all = gathered[:, :half]
    grad_gate_all = gathered[:, half : 2 * half]
    grad_upper_all = gathered[:, 2 * half : 3 * half]
    slope_all = gathered[:, 3 * half].astype(F32) + gathered[:, 3 * half + 1].astype(F32)
    input_part = right_transpose(grad_gate_all, gate_half) + right_transpose(
        grad_upper_all, up_half
    )
    input_sum = lax.psum_scatter(
        input_part.astype(BF), token_axes, scatter_dimension=0, tiled=True
    ).astype(F32)
    place = (lax.axis_index("col") * 2 + core) * tokens
    own_slope = lax.dynamic_slice_in_dim(slope_all, place, tokens, 0)
    input_grad = upstream.astype(F32) + own_slope[:, None] * head_value[None, :] + input_sum
    grad_mixed = (upstream_all.astype(F32) + slope_all[:, None] * head_value[None, :]).astype(BF)
    down_grad = transpose_product(hidden_all, grad_mixed)

    def both_halves(part):
        keep = lax.dynamic_slice_in_dim(part, core * (depth // 2), depth // 2, 0)
        send = lax.dynamic_slice_in_dim(part, (1 - core) * (depth // 2), depth // 2, 0)
        other = lax.ppermute(send.astype(BF), "dp", [(0, 1), (1, 0)]).astype(F32)
        first = core == 0
        return jnp.concatenate(
            [jnp.where(first, keep, other), jnp.where(first, other, keep)], axis=1
        )

    gate_grad = both_halves(transpose_product(x_all, grad_gate_all))
    up_grad = both_halves(transpose_product(x_all, grad_upper_all))
    return (gate_grad, up_grad, down_grad, input_grad)


def solution(mesh):
    in_specs = (
        P(("col", "dp"), "row"),
        P("row", "col"),
        P("row", "col"),
        P("col", "row"),
        P("row"),
        P(("col", "dp"), "row"),
        P(("col", "dp")),
        P(("col", "dp")),
    )
    out_specs = (
        P(("row", "dp"), "col"),
        P(("row", "dp"), "col"),
        P(("col", "dp"), "row"),
        P(("col", "dp"), "row"),
    )
    return jax.shard_map(
        per_device, mesh=mesh, in_specs=in_specs, out_specs=out_specs, check_vma=False
    )
```

profile of v0, /device:TPU:0, one launch (start us, length us, event | category | flops | bytes accessed | tf_op | source)
XLA Modules:
  0.0 312.7 jit_solution(9628465307973189131)
XLA Ops:
  7.2 0.0 all-gather.3.cloned.1.call-start
  7.2 0.7 convert_bitcast_fusion.2
  7.9 0.1 copy.22
  8.0 1.7 fusion.37
  9.7 0.0 all-gather.3.cloned.1.call-update
  9.8 0.0 reduce-scatter.3.cloned.1.call-start
  9.8 0.7 reshape.23
  10.5 2.1 fusion.22
  12.6 0.1 reshape.22
  12.7 25.9 %all-gather.3.cloned.1.call-done = bf16[1024,1152]{1,0:T(8,128)(2,1)} async-done(((bf16[128,1152]{1,0:T(8,128)(2,1)}), bf16[1024,1152]{1,0:T(8,128)(2,1)}) %all-gather.3.cloned.1.call-update) | async-done | bytes 2359312 | tf_op jit(solution)/shard_map/all_gather | solution.py:31
  38.6 1.6 fusion.33
  40.2 0.2 broadcast_in_dim.14
  40.4 0.0 copy-start
  40.4 0.0 copy-start.4
  40.4 5.9 %convolution_convert_fusion = bf16[1024,1792]{1,0:T(8,128)(2,1)} fusion(bf16[3584,512]{1,0:T(8,128)(2,1)} %param.11, s32[]{:T(128)S(6)} %select_n.40, bf16[1024,1152]{1,0:T(8,128)(2,1)} %all-gather.3.cloned.1.call-done), kind=kOutput, calls=%fused_computation | convolution fusion | flops 1880883200 | bytes 6553604 | tf_op jit(solution)/shard_map/dot_general | solution.py:16
  46.3 0.0 copy-done
  46.4 0.0 copy-done.4
  46.4 3.9 %convolution_convert_fusion.1 = bf16[1024,1792]{1,0:T(8,128)(2,1)} fusion(bf16[512,3584]{1,0:T(8,128)(2,1)S(1)} %copy-done.4, s32[]{:T(128)S(6)} %select_n.40, bf16[1024,1152]{1,0:T(8,128)(2,1)S(1)} %copy-done), kind=kOutput, calls=%fused_computation.1 | convolution fusion | flops 1880883200 | bytes 6553604 | tf_op jit(solution)/shard_map/dot_general | solution.py:54
  50.3 0.0 copy-done.5
  50.3 3.9 %convolution_convert_fusion.2 = bf16[1024,1792]{1,0:T(8,128)(2,1)} fusion(bf16[512,3584]{1,0:T(8,128)(2,1)S(1)} %copy-done.5, s32[]{:T(128)S(6)} %select_n.40, bf16[1024,1152]{1,0:T(8,128)(2,1)S(1)} %copy-done), kind=kOutput, calls=%fused_computation.2 | convolution fusion | flops 1880883200 | bytes 6553604 | tf_op jit(solution)/shard_map/dot_general | solution.py:53
  54.3 18.4 %concatenate.19 = bf16[1024,5504]{1,0:T(8,128)(2,1)} concatenate(bf16[1024,1792]{1,0:T(8,128)(2,1)} %convolution_convert_fusion.2, bf16[1024,1792]{1,0:T(8,128)(2,1)} %convolution_convert_fusion.1, bf16[1024,1792]{1,0:T(8,128)(2,1)} %convolution_convert_fusion, bf16[1024,1]{1,0:T(8,128)(2,1)S(1)} %broadcast_in_dim.14, bf16[1024,28]{1,0:T(8,128)(2,1)S(1)} %bitcast.12, ...), dimensions={1} | concatenate | bytes 22544384 | tf_op jit(solution)/shard_map/concatenate | solution.py:51
  72.6 0.0 reduce-scatter.3.cloned.1.call-update
  72.7 0.0 all-gather.5.cloned.1.call-start
  72.7 0.9 slice-done
  73.6 0.2 slice_reduce_fusion
  73.8 90.5 %reduce-scatter.3.cloned.1.call-done = bf16[64,5504]{1,0:T(8,128)(2,1)} async-done(((bf16[1024,5504]{1,0:T(8,128)(2,1)}), bf16[64,5504]{1,0:T(8,128)(2,1)}) %reduce-scatter.3.cloned.1.call-update) | async-done | bytes 704528 | tf_op jit(solution)/shard_map/reduce_scatter | solution.py:60
  164.3 0.8 slice.71
  165.1 0.1 mul.114
  165.2 1.2 convert_element_type.87
  166.4 0.1 slice_reduce_fusion.1
  166.5 0.0 copy-start.3
  166.5 0.2 multiply_reduce_fusion
  166.8 14.2 %psum.7 = f32[64]{0:T(128)S(1)} all-reduce(f32[64]{0:T(128)S(1)} %get-tuple-element.8), channel_id=1, replica_groups=mesh['row'=16,'col'=4,'dp'=2] {'col','dp'}, use_global_device_ids=true, to_apply=%region_2.3 | all-reduce | flops 64 | bytes 512 | tf_op jit(solution)/shard_map/psum | solution.py:68
  181.0 0.3 multiply_convert_fusion.1
  181.3 0.1 copy.21
  181.4 0.9 fusion.29
  182.3 0.0 all-gather.5.cloned.1.call-update
  182.3 0.0 reduce-scatter.5.cloned.1.call-start
  182.4 0.0 copy-done.3
  182.4 80.0 %all-gather.5.cloned.1.call-done = bf16[1024,5504]{1,0:T(8,128)(2,1)} async-done(((bf16[64,5504]{1,0:T(8,128)(2,1)}), bf16[1024,5504]{1,0:T(8,128)(2,1)}) %all-gather.5.cloned.1.call-update) | async-done | bytes 11272208 | tf_op jit(solution)/shard_map/all_gather | solution.py:81
  262.4 4.8 %fusion.2 = f32[1024,512]{1,0:T(8,128)S(1)} fusion(bf16[1024,5504]{1,0:T(8,128)(2,1)} %all-gather.5.cloned.1.call-done, bf16[512,3584]{1,0:T(8,128)(2,1)} %param.10, s32[]{:T(128)S(6)} %select_n.40), kind=kOutput, calls=%fused_computation.7 | convolution fusion | flops 1879048192 | bytes 7602180 | tf_op jit(solution)/shard_map/dot_general | solution.py:16
  267.2 0.0 copy-done.6
  267.2 0.0 copy-start.1
  267.3 5.2 %add_convert_fusion = bf16[1024,512]{1,0:T(8,128)(2,1)} fusion(f32[1024,512]{1,0:T(8,128)S(1)} %fusion.2, bf16[512,3584]{1,0:T(8,128)(2,1)S(1)} %copy-done.6, s32[]{:T(128)S(6)} %select_n.40, bf16[1024,5504]{1,0:T(8,128)(2,1)} %all-gather.5.cloned.1.call-done), kind=kOutput, calls=%fused_computation.19 | convolution fusion | flops 1880096768 | bytes 8650756 | tf_op jit(solution)/shard_map/dot_general | solution.py:16
  272.5 0.0 reduce-scatter.5.cloned.1.call-update
  272.5 0.0 copy-done.1
  272.5 4.2 %fusion.4 = f32[512,1792]{1,0:T(8,128)S(1)} fusion(bf16[1024,5504]{1,0:T(8,128)(2,1)} %all-gather.5.cloned.1.call-done, bf16[1024,1152]{1,0:T(8,128)(2,1)S(1)} %copy-done.1), kind=kOutput, calls=%fused_computation.9 | convolution fusion | flops 1879048192 | bytes 8388608 | tf_op jit(solution)/shard_map/dot_general | solution.py:12
  276.7 0.1 dynamic-slice_convert_fusion
  276.8 0.3 collective-permute-start.1
  277.1 4.1 %fusion.8 = f32[512,1792]{1,0:T(8,128)S(1)} fusion(bf16[1024,5504]{1,0:T(8,128)(2,1)} %all-gather.5.cloned.1.call-done, bf16[1024,1152]{1,0:T(8,128)(2,1)S(1)} %copy-done.1), kind=kOutput, calls=%fused_computation.13 | convolution fusion | flops 1879048192 | bytes 8388608 | tf_op jit(solution)/shard_map/dot_general | solution.py:12
  281.2 0.1 dynamic-slice_convert_fusion.1
  281.3 0.6 collective-permute-start
  281.9 1.5 convert_add_fusion
  283.4 0.1 dynamic-slice_reduce_fusion
  283.6 6.1 %fusion = f32[1792,512]{1,0:T(8,128)} fusion(bf16[1024,5504]{1,0:T(8,128)(2,1)} %all-gather.5.cloned.1.call-done, f32[512]{0:T(512)S(1)} %convert_element_type.103, f32[1024]{0:T(1024)S(1)} %get-tuple-element.11, bf16[1024,1152]{1,0:T(8,128)(2,1)S(1)} %copy-done.1), kind=kOutput, calls=%fused_computation.3 | convolution fusion | flops 1881145344 | bytes 8394752 | tf_op jit(solution)/shard_map/dot_general | solution.py:12
  289.6 0.0 collective-permute-done.1
  289.6 0.3 convert_select_fusion.1
  289.9 2.3 pad_maximum_fusion.1
  292.2 0.0 collective-permute-done
  292.2 0.2 convert_select_fusion.3
  292.5 0.0 copy-start.2
  292.5 2.3 pad_maximum_fusion
  294.8 9.6 %reduce-scatter.5.cloned.1.call-done = bf16[128,512]{1,0:T(8,128)(2,1)} async-done(((bf16[1024,512]{1,0:T(8,128)(2,1)}), bf16[128,512]{1,0:T(8,128)(2,1)}) %reduce-scatter.5.cloned.1.call-update) | async-done | bytes 131088 | tf_op jit(solution)/shard_map/reduce_scatter | solution.py:91
  304.4 1.7 convert_add_fusion.1
  (13 shorter events, 0.1 us)
Async XLA Ops:
  7.2 31.4 %all-gather.3.cloned.1.call-start = ((), (), s32[]{:S(2)}) async-start(), calls=%async_computation.2 | async-start | bytes 2654208 | tf_op jit(solution)/shard_map/all_gather | solution.py:31
  9.8 154.5 %reduce-scatter.3.cloned.1.call-start = ((), (), s32[]{:S(2)}) async-start(), calls=%async_computation.3 | async-start | bytes 11976704 | tf_op jit(solution)/shard_map/reduce_scatter | solution.py:60
  40.4 5.9 %copy-start = (bf16[1024,1152]{1,0:T(8,128)(2,1)S(1)}, bf16[1024,1152]{1,0:T(8,128)(2,1)}, u32[]{:S(2)}) copy-start(bf16[1024,1152]{1,0:T(8,128)(2,1)} %all-gather.3.cloned.1.call-done) | copy-start | bytes 7077892
  40.4 5.9 %copy-start.4 = (bf16[512,3584]{1,0:T(8,128)(2,1)S(1)}, bf16[512,3584]{1,0:T(8,128)(2,1)}, u32[]{:S(2)}) copy-start(bf16[512,3584]{1,0:T(8,128)(2,1)} %param.10) | copy-start | bytes 11010052
  46.4 3.9 %copy-start.5 = (bf16[512,3584]{1,0:T(8,128)(2,1)S(1)}, bf16[512,3584]{1,0:T(8,128)(2,1)}, u32[]{:S(2)}) copy-start(bf16[512,3584]{1,0:T(8,128)(2,1)} %param.9) | copy-start | bytes 11010052
  72.6 0.9 slice-start
  72.7 189.7 %all-gather.5.cloned.1.call-start = ((), (), s32[]{:S(2)}) async-start(), calls=%async_computation.4 | async-start | bytes 11976704 | tf_op jit(solution)/shard_map/all_gather | solution.py:81
  166.5 15.9 %copy-start.3 = (bf16[512]{0:T(512)(128)(2,1)S(1)}, bf16[512]{0:T(512)(128)(2,1)}, u32[]{:S(2)}) copy-start(bf16[512]{0:T(512)(128)(2,1)} %param.12) | copy-start | bytes 3076
  182.3 122.1 %reduce-scatter.5.cloned.1.call-start = ((), (), s32[]{:S(2)}) async-start(), calls=%async_computation.5 | async-start | bytes 1179648 | tf_op jit(solution)/shard_map/reduce_scatter | solution.py:91
  262.4 4.9 %copy-start.6 = (bf16[512,3584]{1,0:T(8,128)(2,1)S(1)}, bf16[512,3584]{1,0:T(8,128)(2,1)}, u32[]{:S(2)}) copy-start(bf16[512,3584]{1,0:T(8,128)(2,1)} %param.9) | copy-start | bytes 11010052
  267.2 5.3 %copy-start.1 = (bf16[1024,1152]{1,0:T(8,128)(2,1)S(1)}, bf16[1024,1152]{1,0:T(8,128)(2,1)}, u32[]{:S(2)}) copy-start(bf16[1024,1152]{1,0:T(8,128)(2,1)} %all-gather.3.cloned.1.call-done) | copy-start | bytes 7077892
  276.8 12.8 %collective-permute-start.1 = (bf16[256,1792]{1,0:T(8,128)(2,1)S(1)}, bf16[256,1792]{1,0:T(8,128)(2,1)S(1)}, u32[]{:S(2)}, u32[]{:S(2)}) collective-permute-start(bf16[256,1792]{1,0:T(8,128)(2,1)S(1)} %dynamic-slice_convert_fusion), channel_id=1, source_target_pairs={{0,1},{1,0},{2,3},{3,2},{4,5},{5,4},{6,7},{7,6},{8,9},{9,8},{10,11... | collective-permute-start | bytes 2752520 | tf_op jit(solution)/shard_map/ppermute | solution.py:103
  281.3 10.9 %collective-permute-start = (bf16[256,1792]{1,0:T(8,128)(2,1)S(1)}, bf16[256,1792]{1,0:T(8,128)(2,1)S(1)}, u32[]{:S(2)}, u32[]{:S(2)}) collective-permute-start(bf16[256,1792]{1,0:T(8,128)(2,1)S(1)} %dynamic-slice_convert_fusion.1), channel_id=1, source_target_pairs={{0,1},{1,0},{2,3},{3,2},{4,5},{5,4},{6,7},{7,6},{8,9},{9,8},{10,11... | collective-permute-start | bytes 2752520 | tf_op jit(solution)/shard_map/ppermute | solution.py:103
  292.5 12.0 %copy-start.2 = (bf16[128,512]{1,0:T(8,128)(2,1)S(1)}, bf16[128,512]{1,0:T(8,128)(2,1)}, u32[]{:S(2)}) copy-start(bf16[128,512]{1,0:T(8,128)(2,1)} %param.13) | copy-start | bytes 393220
Sparse Core Ops, SparseCore 0:
  10.3 28.2 all-gather.2
  72.8 91.4 reduce-scatter.2
  182.4 79.9 all-gather.4
  272.6 31.7 reduce-scatter.4
where the time goes:
time: 314 us; the launch traced here: 313 us
  waiting for transfers between devices  206 us (66%)
  matrix products  41.9 us (13%)
  local copies, waits for them, and re-layouts  21.9 us (7%)
  blocking collectives  14.2 us (5%)
  between operations  14 us (4%)
  other arithmetic  13.6 us (4%)
    reduce_scatter x1, waiting for transfers between devices, per_device(): lax.psum_scatter(partial, 'row', scatter_dimension=0, tiled=True)  90.5 us
    all_gather x1, waiting for transfers between devices, per_device(): lax.all_gather(jnp.concatenate([hidden, grad_gate, grad_upper, slopes], a...  80 us
    all_gather x1, waiting for transfers between devices, per_device(): everyone = lax.all_gather(packed, token_axes, axis=0, tiled=True)  25.9 us
    concatenate x1, local copies, waits for them, and re-layouts, per_device(): jnp.concatenate([jnp.dot(x_all, gate_half, preferred_element_type=F32).as...  18.4 us
    dot_general x3, matrix products, right_transpose(): lax.dot_general(left, right, (((1,), (1,)), ((), ())), preferred_element_...  16 us
    dot_general x3, matrix products, transpose_product(): lax.dot_general(left, right, (((0,), (0,)), ((), ())), preferred_element_...  14.4 us
    psum x1, blocking collectives, per_device(): lax.psum(jnp.sum(hidden.astype(F32) * head_hidden[None, :], axis=1), toke...  14.2 us
    reduce_scatter x1, waiting for transfers between devices, per_device(): lax.psum_scatter(input_part.astype(BF), token_axes, scatter_dimension=0,...  9.63 us
  transfers between devices with their start and end apart: 6, of which 4 were waited for; matrix products, arithmetic and copies ran while one was open for 8% of the time, Pallas kernels for 0%

commit v1 on v0

--- a/solution.py
+++ b/solution.py
@@ -65,8 +65,9 @@
     head_hidden = extra[:, 1 : 1 + per_token].reshape(half)
     sigmoid_gate = jax.nn.sigmoid(gate)
     hidden = (gate * sigmoid_gate * upper).astype(BF)
-    score = extra[:, 0] + lax.psum(
-        jnp.sum(hidden.astype(F32) * head_hidden[None, :], axis=1), token_axes
+    score = extra[:, 0] + jnp.sum(
+        lax.all_gather(jnp.sum(hidden.astype(F32) * head_hidden[None, :], axis=1), token_axes),
+        axis=0,
     )
     own_tags = lax.dynamic_slice_in_dim(everyone[:, 2 * depth :], row * mine, mine, 0).astype(F32)
     slope = reward_weight * own_tags[:, 1] * (jax.nn.sigmoid(score) - own_tags[:, 0])

time: 314 us -> 323 us (1.029)
  local copies, waits for them, and re-layouts: 21.9 us -> 28.5 us
    reduce_scatter x1 -> x0, waiting for transfers between devices: 90.5 us -> none  [per_device(): lax.psum_scatter(partial, 'row', scatter_dimension=0, tiled=True)]
    unnamed x4 -> x5, waiting for transfers between devices: 0.07 us -> 89.9 us
    unnamed x0 -> x1, blocking collectives: none -> 14.2 us
    psum x1 -> x0, blocking collectives: 14.2 us -> none  [per_device(): lax.psum(jnp.sum(hidden.astype(F32) * head_hidden[None, :], axis=1), toke...]
    unnamed x16 -> x25, local copies, waits for them, and re-layouts: 0.86 us -> 7.34 us
where the time goes in v1:
time: 323 us; the launch traced here: 322 us
  waiting for transfers between devices  208 us (64%)
  matrix products  41.8 us (13%)
  local copies, waits for them, and re-layouts  28.5 us (9%)
  between operations  14.7 us (5%)
  blocking collectives  14.2 us (4%)
  other arithmetic  13.9 us (4%)
    unnamed x5, waiting for transfers between devices  89.9 us
    all_gather x1, waiting for transfers between devices, per_device(): lax.all_gather(jnp.concatenate([hidden, grad_gate, grad_upper, slopes], a...  79.7 us
    all_gather x1, waiting for transfers between devices, per_device(): everyone = lax.all_gather(packed, token_axes, axis=0, tiled=True)  28.2 us
    concatenate x1, local copies, waits for them, and re-layouts, per_device(): jnp.concatenate([jnp.dot(x_all, gate_half, preferred_element_type=F32).as...  18.3 us
    dot_general x3, matrix products, right_transpose(): lax.dot_general(left, right, (((1,), (1,)), ((), ())), preferred_element_...  16 us
    dot_general x3, matrix products, transpose_product(): lax.dot_general(left, right, (((0,), (0,)), ((), ())), preferred_element_...  14.3 us
    unnamed x1, blocking collectives  14.2 us
    reduce_scatter x1, waiting for transfers between devices, per_device(): lax.psum_scatter(input_part.astype(BF), token_axes, scatter_dimension=0,...  10.1 us
  transfers between devices with their start and end apart: 6, of which 4 were waited for; matrix products, arithmetic and copies ran while one was open for 8% of the time, Pallas kernels for 0%

profile of v1, /device:TPU:0, one launch (start us, length us, event | category | flops | bytes accessed | tf_op | source)
XLA Modules:
  0.0 322.0 jit_solution(10862935364537663238)
XLA Ops:
  7.2 0.0 all-gather.4.cloned.1.call-start
  7.2 1.0 copy.35
  8.2 1.0 copy.36
  9.3 0.7 convert_bitcast_fusion
  10.0 0.7 pad_maximum_fusion.3
  10.7 0.0 all-gather.4.cloned.1.call-update
  10.7 0.0 reduce-scatter.7.cloned.1.call-start
  10.8 0.7 reshape.29
  11.5 2.1 fusion.21
  13.6 0.1 reshape.22
  13.7 28.2 %all-gather.4.cloned.1.call-done = bf16[1024,1152]{0,1:T(8,128)(2,1)} async-done(((bf16[128,1152]{0,1:T(8,128)(2,1)}), bf16[1024,1152]{0,1:T(8,128)(2,1)}) %all-gather.4.cloned.1.call-update) | async-done | bytes 2359312 | tf_op jit(solution)/shard_map/all_gather | solution.py:31
  41.9 1.5 fusion.30
  43.4 0.2 broadcast_in_dim.14
  43.6 0.0 copy-start.5
  43.6 5.9 %convolution_convert_fusion = bf16[1024,1792]{1,0:T(8,128)(2,1)} fusion(bf16[3584,512]{1,0:T(8,128)(2,1)} %param.11, s32[]{:T(128)S(6)} %select_n.40, bf16[1024,1152]{0,1:T(8,128)(2,1)} %all-gather.4.cloned.1.call-done), kind=kOutput, calls=%fused_computation | convolution fusion | flops 1880883200 | bytes 6553604 | tf_op jit(solution)/shard_map/dot_general | solution.py:16
  49.6 4.0 %convolution_convert_fusion.1 = bf16[1024,1792]{1,0:T(8,128)(2,1)} fusion(bf16[512,3584]{1,0:T(8,128)(2,1)S(1)} %copy-done.5, s32[]{:T(128)S(6)} %select_n.40, bf16[1024,1152]{0,1:T(8,128)(2,1)S(1)} %copy-done.2), kind=kOutput, calls=%fused_computation.1 | convolution fusion | flops 1880883200 | bytes 6553604 | tf_op jit(solution)/shard_map/dot_general | solution.py:54
  53.5 0.0 copy-done.6
  53.5 3.9 %convolution_convert_fusion.2 = bf16[1024,1792]{1,0:T(8,128)(2,1)} fusion(bf16[512,3584]{1,0:T(8,128)(2,1)S(1)} %copy-done.6, s32[]{:T(128)S(6)} %select_n.40, bf16[1024,1152]{0,1:T(8,128)(2,1)S(1)} %copy-done.2), kind=kOutput, calls=%fused_computation.2 | convolution fusion | flops 1880883200 | bytes 6553604 | tf_op jit(solution)/shard_map/dot_general | solution.py:53
  57.6 18.3 %concatenate.19 = bf16[1024,5504]{1,0:T(8,128)(2,1)} concatenate(bf16[1024,1792]{1,0:T(8,128)(2,1)} %convolution_convert_fusion.2, bf16[1024,1792]{1,0:T(8,128)(2,1)} %convolution_convert_fusion.1, bf16[1024,1792]{1,0:T(8,128)(2,1)} %convolution_convert_fusion, bf16[1024,1]{1,0:T(8,128)(2,1)S(1)} %broadcast_in_dim.14, bf16[1024,28]{1,0:T(8,128)(2,1)S(1)} %bitcast.16, ...), dimensions={1} | concatenate | bytes 22544384 | tf_op jit(solution)/shard_map/concatenate | solution.py:51
  75.9 0.0 reduce-scatter.7.cloned.1.call-update
  75.9 0.0 all-gather.6.cloned.1.call-start
  76.0 0.6 copy-done.8
  76.5 0.6 dynamic-slice.1
  77.8 0.7 dynamic-slice_convert_fusion.2
  78.5 89.8 %reduce-scatter.7.cloned.1.call-done = bf16[64,5504]{1,0:T(8,128)(2,1)} async-done(((bf16[1024,5504]{1,0:T(8,128)(2,1)}), bf16[64,5504]{1,0:T(8,128)(2,1)}) %reduce-scatter.7.cloned.1.call-update) | async-done | bytes 704528
  168.3 2.1 copy.42
  170.4 0.0 copy-start
  170.4 1.1 copy-done
  171.5 1.5 convert_element_type.91
  173.0 0.1 copy.39
  173.1 0.1 mul.118
  173.2 0.4 multiply_reduce_fusion
  173.6 0.2 dynamic-update-slice
  173.8 14.2 %all-reduce.2 = f32[512]{0:T(512)S(1)} all-reduce(f32[512]{0:T(512)S(1)} %dynamic-update-slice), channel_id=2, replica_groups=mesh['row'=16,'col'=4,'dp'=2] {'col','dp'}, use_global_device_ids=true, to_apply=%add.2 | all-reduce | flops 512 | bytes 4096
  188.1 0.1 reshape.23
  188.2 0.8 fusion.49
  188.9 0.5 multiply_convert_fusion.1
  189.5 0.0 copy-start.4
  189.5 0.3 pad_maximum_fusion.2
  189.8 1.8 copy.40
  191.6 0.0 all-gather.6.cloned.1.call-update
  191.6 0.2 reduce-scatter.5.cloned.1.call-start
  191.9 79.7 %all-gather.6.cloned.1.call-done = bf16[1024,5504]{1,0:T(8,128)(2,1)} async-done(((bf16[64,5504]{1,0:T(8,128)(2,1)}), bf16[1024,5504]{1,0:T(8,128)(2,1)}) %all-gather.6.cloned.1.call-update) | async-done | bytes 11272208 | tf_op jit(solution)/shard_map/all_gather | solution.py:82
  271.6 4.8 %fusion.2 = f32[1024,512]{1,0:T(8,128)S(1)} fusion(bf16[1024,5504]{1,0:T(8,128)(2,1)} %all-gather.6.cloned.1.call-done, bf16[512,3584]{1,0:T(8,128)(2,1)} %param.10, s32[]{:T(128)S(6)} %select_n.40), kind=kOutput, calls=%fused_computation.7 | convolution fusion | flops 1879048192 | bytes 7602180 | tf_op jit(solution)/shard_map/dot_general | solution.py:16
  276.5 5.3 %add_convert_fusion = bf16[1024,512]{1,0:T(8,128)(2,1)} fusion(f32[1024,512]{1,0:T(8,128)S(1)} %fusion.2, bf16[512,3584]{1,0:T(8,128)(2,1)S(1)} %copy-done.7, s32[]{:T(128)S(6)} %select_n.40, bf16[1024,5504]{1,0:T(8,128)(2,1)} %all-gather.6.cloned.1.call-done), kind=kOutput, calls=%fused_computation.19 | convolution fusion | flops 1880096768 | bytes 8650756 | tf_op jit(solution)/shard_map/dot_general | solution.py:16
  281.7 0.0 reduce-scatter.5.cloned.1.call-update
  281.8 4.1 %fusion.4 = f32[512,1792]{1,0:T(8,128)S(1)} fusion(bf16[1024,5504]{1,0:T(8,128)(2,1)} %all-gather.6.cloned.1.call-done, bf16[1024,1152]{0,1:T(8,128)(2,1)S(1)} %copy-done.3), kind=kOutput, calls=%fused_computation.9 | convolution fusion | flops 1879048192 | bytes 8388608 | tf_op jit(solution)/shard_map/dot_general | solution.py:12
  285.9 0.1 dynamic-slice_convert_fusion
  286.0 0.1 collective-permute-start.1
  286.1 4.1 %fusion.8 = f32[512,1792]{1,0:T(8,128)S(1)} fusion(bf16[1024,5504]{1,0:T(8,128)(2,1)} %all-gather.6.cloned.1.call-done, bf16[1024,1152]{0,1:T(8,128)(2,1)S(1)} %copy-done.3), kind=kOutput, calls=%fused_computation.13 | convolution fusion | flops 1879048192 | bytes 8388608 | tf_op jit(solution)/shard_map/dot_general | solution.py:12
  290.2 0.1 dynamic-slice_convert_fusion.1
  290.3 0.6 collective-permute-start
  290.9 1.4 convert_add_fusion
  292.3 0.1 dynamic-slice_reduce_fusion
  292.4 6.1 %fusion = f32[1792,512]{1,0:T(8,128)} fusion(bf16[1024,5504]{1,0:T(8,128)(2,1)} %all-gather.6.cloned.1.call-done, f32[512]{0:T(512)S(1)} %convert_element_type.107, f32[1024]{0:T(1024)S(1)} %get-tuple-element.9, bf16[1024,1152]{0,1:T(8,128)(2,1)S(1)} %copy-done.3), kind=kOutput, calls=%fused_computation.3 | convolution fusion | flops 1881145344 | bytes 8394752 | tf_op jit(solution)/shard_map/dot_general | solution.py:12
  298.5 0.0 collective-permute-done.1
  298.5 0.3 convert_select_fusion.1
  298.8 2.3 pad_maximum_fusion.1
  301.1 0.0 collective-permute-done
  301.1 0.2 convert_select_fusion.3
  301.3 0.0 copy-start.1
  301.3 2.3 pad_maximum_fusion
  303.7 10.1 %reduce-scatter.5.cloned.1.call-done = bf16[128,512]{1,0:T(8,128)(2,1)} async-done(((bf16[1024,512]{1,0:T(8,128)(2,1)}), bf16[128,512]{1,0:T(8,128)(2,1)}) %reduce-scatter.5.cloned.1.call-update) | async-done | bytes 131088 | tf_op jit(solution)/shard_map/reduce_scatter | solution.py:92
  313.8 1.7 convert_add_fusion.1
  (23 shorter events, 0.2 us)
Async XLA Ops:
  7.2 34.7 %all-gather.4.cloned.1.call-start = ((), (), s32[]{:S(2)}) async-start(), calls=%async_computation.2 | async-start | bytes 2654208 | tf_op jit(solution)/shard_map/all_gather | solution.py:31
  10.7 157.6 %reduce-scatter.7.cloned.1.call-start = ((), (), s32[]{:S(2)}) async-start(), calls=%async_computation.5 | async-start | bytes 11976704
  43.6 6.0 %copy-start.2 = (bf16[1024,1152]{0,1:T(8,128)(2,1)S(1)}, bf16[1024,1152]{0,1:T(8,128)(2,1)}, u32[]{:S(2)}) copy-start(bf16[1024,1152]{0,1:T(8,128)(2,1)} %all-gather.4.cloned.1.call-done) | copy-start | bytes 7077892
  43.6 5.9 %copy-start.5 = (bf16[512,3584]{1,0:T(8,128)(2,1)S(1)}, bf16[512,3584]{1,0:T(8,128)(2,1)}, u32[]{:S(2)}) copy-start(bf16[512,3584]{1,0:T(8,128)(2,1)} %param.10) | copy-start | bytes 11010052
  49.6 4.0 %copy-start.6 = (bf16[512,3584]{1,0:T(8,128)(2,1)S(1)}, bf16[512,3584]{1,0:T(8,128)(2,1)}, u32[]{:S(2)}) copy-start(bf16[512,3584]{1,0:T(8,128)(2,1)} %param.9) | copy-start | bytes 11010052
  75.9 0.7 copy-start.8
  75.9 1.9 slice-start
  75.9 195.7 %all-gather.6.cloned.1.call-start = ((), (), s32[]{:S(2)}) async-start(), calls=%async_computation.3 | async-start | bytes 11976704 | tf_op jit(solution)/shard_map/all_gather | solution.py:82
  170.4 1.1 copy-start
  189.5 2.4 copy-start.4
  191.6 122.1 %reduce-scatter.5.cloned.1.call-start = ((), (), s32[]{:S(2)}) async-start(), calls=%async_computation.4 | async-start | bytes 1179648 | tf_op jit(solution)/shard_map/reduce_scatter | solution.py:92
  271.6 4.9 %copy-start.7 = (bf16[512,3584]{1,0:T(8,128)(2,1)S(1)}, bf16[512,3584]{1,0:T(8,128)(2,1)}, u32[]{:S(2)}) copy-start(bf16[512,3584]{1,0:T(8,128)(2,1)} %param.9) | copy-start | bytes 11010052
  276.5 5.3 %copy-start.3 = (bf16[1024,1152]{0,1:T(8,128)(2,1)S(1)}, bf16[1024,1152]{0,1:T(8,128)(2,1)}, u32[]{:S(2)}) copy-start(bf16[1024,1152]{0,1:T(8,128)(2,1)} %all-gather.4.cloned.1.call-done) | copy-start | bytes 7077892
  286.0 12.5 %collective-permute-start.1 = (bf16[256,1792]{1,0:T(8,128)(2,1)S(1)}, bf16[256,1792]{1,0:T(8,128)(2,1)S(1)}, u32[]{:S(2)}, u32[]{:S(2)}) collective-permute-start(bf16[256,1792]{1,0:T(8,128)(2,1)S(1)} %dynamic-slice_convert_fusion), channel_id=1, source_target_pairs={{0,1},{1,0},{2,3},{3,2},{4,5},{5,4},{6,7},{7,6},{8,9},{9,8},{10,11... | collective-permute-start | bytes 2752520 | tf_op jit(solution)/shard_map/ppermute | solution.py:104
  290.3 10.8 %collective-permute-start = (bf16[256,1792]{1,0:T(8,128)(2,1)S(1)}, bf16[256,1792]{1,0:T(8,128)(2,1)S(1)}, u32[]{:S(2)}, u32[]{:S(2)}) collective-permute-start(bf16[256,1792]{1,0:T(8,128)(2,1)S(1)} %dynamic-slice_convert_fusion.1), channel_id=1, source_target_pairs={{0,1},{1,0},{2,3},{3,2},{4,5},{5,4},{6,7},{7,6},{8,9},{9,8},{10,11... | collective-permute-start | bytes 2752520 | tf_op jit(solution)/shard_map/ppermute | solution.py:104
  301.3 12.4 %copy-start.1 = (bf16[128,512]{1,0:T(8,128)(2,1)S(1)}, bf16[128,512]{1,0:T(8,128)(2,1)}, u32[]{:S(2)}) copy-start(bf16[128,512]{1,0:T(8,128)(2,1)} %param.13) | copy-start | bytes 393220
Sparse Core Ops, SparseCore 0:
  10.8 31.0 all-gather.3
  76.0 92.2 reduce-scatter.6
  191.7 79.8 all-gather.5
  281.9 31.8 reduce-scatter.4
